TPU v7x, 32 devices: a whole 2x2x4 slice. The times are simulated.
32 devices in a mesh: dp: 4 (over z), dom: 8 (over y, x, core).
Axes of the slice: x: 2, y: 2, z: 4, core: 2. Of those that a mesh axis runs over, the one named last changes fastest.
Arguments:
- feats: bfloat16 [4096, 1024], P(('dp', 'dom')), parts along dimension 0, may hold values from -26 to 26
- adj_own: int32 [4096, 128], P(('dp', 'dom')), parts along dimension 0, may hold values 0 or 1
- adj_prev: int32 [4096, 32], P(('dp', 'dom')), parts along dimension 0, may hold values 0 or 1
- adj_next: int32 [4096, 32], P(('dp', 'dom')), parts along dimension 0, may hold values 0 or 1
- bcount: int32 [32, 2], P('dp'), parts along dimension 0, may hold values from 1 to 32
- wqkv: bfloat16 [3, 1024, 1024], P(None, None, 'dom'), may hold values from -1 to 1, as said below
- w_mp: bfloat16 [1024, 1024], P('dom'), may hold values from -0.1875 to 0.1875
- w_out: bfloat16 [1024, 1024], P('dom'), may hold values from -0.1875 to 0.1875
Outputs:
- updated: bfloat16 [4096, 1024], P(('dp', 'dom')), parts along dimension 0
There are 4 independent parts, one for each index of `dp`. A program takes and returns all parts, laid end to end along the dimension named above; an argument that names none is the same for every part. Nothing has to cross between parts.
Inputs may be any that keep to these rules, and one draw needn't show every extreme that they name: `wqkv`: projection weights with entries of deviation about 1024 ** -0.5.
All inputs are finite; a program needn't handle non-finite values. No bound on the sum of `adj_own` or of `adj_prev` or of `adj_next` on one device may be relied on, other than what follows from the above.
Results may differ from a plain program's by a relative error of at most 0.0066.
Values may be sent and summed in bfloat16 or wider, within the bound.
A program may use at most 64 MiB of HBM per device.

v0:
```python
import math

import jax
import jax.numpy as jnp
from jax import lax
from jax.sharding import PartitionSpec as P

HEADS = 32


def with_halo(cells, sides, width):
    for axis, dim in sides:
        count = lax.axis_size(axis)
        ends = count - 1
        head = lax.slice_in_dim(cells, 0, width, axis=dim)
        tail = lax.slice_in_dim(cells, cells.shape[dim] - width, cells.shape[dim], axis=dim)
        cells = jnp.concatenate(
            [
                lax.ppermute(tail, axis, [(i, (i + 1) % count) for i in range(ends)]),
                cells,
                lax.ppermute(head, axis, [((i + 1) % count, i) for i in range(ends)]),
            ],
            axis=dim,
        )
    return cells


def attend(head_qkv, head_size):
    nodes = head_qkv.shape[1]
    columns = head_qkv.shape[2]
    count_heads = columns // head_size
    query = head_qkv[0].reshape(nodes, count_heads, head_size)
    key = head_qkv[1].reshape(nodes, count_heads, head_size)
    value = head_qkv[2].reshape(nodes, count_heads, head_size)
    scale = 1.0 / head_size**0.5
    block = math.gcd(nodes, 512)

    def one_block(index):
        q_block = lax.dynamic_slice_in_dim(query, index * block, block, 0)
        score = jnp.einsum("qhc,khc->hqk", q_block, key, preferred_element_type=jnp.float32) * scale
        peak = jnp.max(score, -1, keepdims=True)
        expo = jnp.exp(score - peak)
        weight = (expo / jnp.sum(expo, -1, keepdims=True)).astype(jnp.bfloat16)
        result = jnp.einsum("hqk,khc->qhc", weight, value, preferred_element_type=jnp.float32)
        return result.astype(jnp.bfloat16).reshape(block, columns)

    blocks = lax.map(one_block, jnp.arange(nodes // block))
    return blocks.reshape(nodes, columns)


def message_term(mixed, w_mp):
    return jnp.dot(
        mixed, lax.all_gather(w_mp, "dom", axis=0, tiled=True), preferred_element_type=jnp.float32
    )


def body(feats, adj_own, adj_prev, adj_next, bcount, wqkv, w_mp, w_out):
    rows = feats.shape[0]
    width = feats.shape[1]
    band = adj_prev.shape[1]
    parts = lax.axis_size("dom")
    myself = lax.axis_index("dom")
    padded = with_halo(feats, (("dom", 0),), band)
    prev_rim = padded[:band]
    next_rim = padded[band + rows :]
    column = jnp.arange(band)
    prev_count = bcount[jnp.maximum(myself - 1, 0), 1]
    next_count = bcount[jnp.minimum(myself + 1, parts - 1), 0]
    prev_vis = (myself > 0) & (column >= band - prev_count)
    next_vis = (myself < parts - 1) & (column < next_count)
    own = adj_own.astype(jnp.bfloat16)
    prv = jnp.where(prev_vis[None, :], adj_prev, 0).astype(jnp.bfloat16)
    nxt = jnp.where(next_vis[None, :], adj_next, 0).astype(jnp.bfloat16)
    degree = (
        1.0
        + jnp.sum(own.astype(jnp.float32), -1)
        + jnp.sum(prv.astype(jnp.float32), -1)
        + jnp.sum(nxt.astype(jnp.float32), -1)
    )
    total = feats.astype(jnp.float32) + jnp.dot(own, feats, preferred_element_type=jnp.float32)
    total = total + jnp.dot(prv, prev_rim, preferred_element_type=jnp.float32)
    total = total + jnp.dot(nxt, next_rim, preferred_element_type=jnp.float32)
    mixed = (total / degree[:, None]).astype(jnp.bfloat16)
    node_qkv = jnp.einsum(
        "nd,tdc->tnc",
        feats,
        lax.all_gather(wqkv, "dom", axis=2, tiled=True),
        preferred_element_type=jnp.float32,
    ).astype(jnp.bfloat16)
    head_qkv = lax.all_to_all(node_qkv, "dom", split_axis=2, concat_axis=1, tiled=True)
    head_out = attend(head_qkv, width // HEADS)
    node_out = lax.all_to_all(head_out, "dom", split_axis=0, concat_axis=1, tiled=True)
    local = message_term(mixed, w_mp)
    attn = jnp.dot(
        node_out,
        lax.all_gather(w_out, "dom", axis=0, tiled=True),
        preferred_element_type=jnp.float32,
    )
    return (feats.astype(jnp.float32) + local + attn).astype(jnp.bfloat16)


def solution(mesh):
    placed = (
        P(("dp", "dom"), None),
        P(("dp", "dom"), None),
        P(("dp", "dom"), None),
        P(("dp", "dom"), None),
        P("dp", None),
        P(None, None, "dom"),
        P("dom", None),
        P("dom", None),
    )
    return jax.shard_map(
        body, mesh=mesh, in_specs=placed, out_specs=P(("dp", "dom"), None), check_vma=False
    )
```

profile of v0, /device:TPU:0, one launch (start us, length us, event | category | flops | bytes accessed | tf_op | source)
XLA Modules:
  0.0 131.9 jit_solution(15720793483775529202)
XLA Ops:
  6.5 2.3 %copy.19 = bf16[3,1024,128]{1,2,0:T(8,128)(2,1)} copy(bf16[3,1024,128]{2,1,0:T(8,128)(2,1)} %param.15) | data formatting | bytes 1572864 | tf_op args[5]
  8.9 0.7 all-gather.4.cloned.1.call-update
  10.4 0.9 fusion.59
  11.3 1.3 collective-permute-start.1
  12.6 3.0 %collective-permute-start = (bf16[32,1024]{1,0:T(8,128)(2,1)S(1)}, bf16[32,1024]{1,0:T(8,128)(2,1)S(1)}, u32[]{:S(2)}, u32[]{:S(2)}) collective-permute-start(bf16[32,1024]{1,0:T(8,128)(2,1)S(1)} %get-tuple-element.53), channel_id=1, source_target_pairs={{0,1},{1,2},{2,3},{3,4},{4,5},{5,6},{6,7},{8,9},{9,10},{10,11},{11... | collective-permute-start | bytes 196616 | tf_op jit(solution)/shard_map/ppermute | solution.py:19
  15.6 1.4 %constant_dynamic-slice_fusion = (s32[1,1]{0,1:T(1,128)}, s32[1,1]{0,1:T(1,128)}) fusion(s32[8,2]{0,1:T(2,128)} %param.14, s32[]{:T(128)S(6)} %max.3, s32[]{:T(128)S(6)} %select_n.15), kind=kLoop, calls=%fused_computation.40 | loop fusion | bytes 24 | tf_op jit(solution)/shard_map/dynamic_slice | solution.py:67
  18.3 0.9 convert_reduce_fusion
  19.2 0.8 convert_reduce_fusion.1
  20.1 37.4 %all-gather.6.cloned.1.call-done = bf16[3,1024,1024]{1,2,0:T(8,128)(2,1)} async-done(((bf16[3,1024,128]{1,2,0:T(8,128)(2,1)}), bf16[3,1024,1024]{1,2,0:T(8,128)(2,1)}) %all-gather.6.cloned.1.call-update) | async-done | bytes 6291472 | tf_op jit(solution)/shard_map/all_gather | solution.py:87
  57.5 4.6 %fusion.44 = bf16[3,128,1024]{1,2,0:T(8,128)(2,1)S(1)} fusion(bf16[3,1024,1024]{1,2,0:T(8,128)(2,1)} %all-gather.6.cloned.1.call-done, bf16[128,1024]{1,0:T(8,128)(2,1)} %param.10), kind=kOutput, calls=%fused_computation.20 | convolution fusion | flops 805699584 | bytes 7340032 | tf_op jit(solution)/shard_map/nd,tdc->tnc/dot_general | solution.py:84
  62.1 1.6 %copy.20 = bf16[3,128,1024]{1,0,2:T(4,128)(2,1)} copy(bf16[3,128,1024]{1,2,0:T(8,128)(2,1)S(1)} %fusion.44) | data formatting | bytes 1572864 | tf_op jit(solution)/shard_map/convert_element_type | solution.py:89
  63.7 3.6 %all-to-all-start = ((bf16[3,128,1024]{1,0,2:T(4,128)(2,1)}), bf16[3,128,1024]{1,0,2:T(4,128)(2,1)S(1)}, u32[]{:S(2)}, u32[]{:S(2)}) async-start(bf16[3,128,1024]{1,0,2:T(4,128)(2,1)} %copy.20), calls=%async_computation | async-start | bytes 2097152 | tf_op jit(solution)/shard_map/all_to_all | solution.py:90
  67.9 16.6 %all-to-all-done = bf16[3,128,1024]{1,0,2:T(4,128)(2,1)S(1)} async-done(((bf16[3,128,1024]{1,0,2:T(4,128)(2,1)}), bf16[3,128,1024]{1,0,2:T(4,128)(2,1)S(1)}, u32[]{:S(2)}, u32[]{:S(2)}) %all-to-all-start) | async-done | bytes 786464 | tf_op jit(solution)/shard_map/all_to_all | solution.py:90
  84.5 1.2 fusion.58
  87.0 16.6 %while.10 = (s32[]{:T(128)}, bf16[2,512,128]{2,1,0:T(8,128)(2,1)}, s32[2]{0:T(128)S(1)}, bf16[1024,4,32]{0,2,1:T(8,128)(2,1)S(1)}, bf16[1024,4,32]{0,2,1:T(8,128...) while((s32[]{:T(128)}, bf16[2,512,128]{2,1,0:T(8,128)(2,1)}, ...), condition=%wide.region_6.7_spmd, body=%wide.region_3.6_spmd.sunk | while | flops 417402880 | bytes 3817699 | solution.py:47
  88.4 3.0 %fusion.86 = f32[4,512]{1,0:T(4,128)S(1)} fusion(bf16[1024,4,32]{0,2,1:T(8,128)(2,1)S(1)} %get-tuple-element.120, bf16[1024,4,32]{0,2,1:T(8,128)(2,1)S(1)} %get-tuple-element.119, s32[]{:T(128)S(6)} %select_n.27), kind=kOutput, calls=%fused_computation.43.clone.1 | convolution fusion | flops 140510208 | bytes 401412 | tf_op jit(solution)/shard_map/while/body/eval_jaxpr/sub | solution.py:42
  91.3 3.1 %fusion.87 = bf16[4,512,32]{1,2,0:T(8,128)(2,1)S(1)} fusion(bf16[1024,4,32]{0,2,1:T(8,128)(2,1)S(1)} %get-tuple-element.121, f32[4,512]{1,0:T(4,128)S(1)} %fusion.86, bf16[1024,4,32]{0,2,1:T(8,128)(2,1)S(1)} %get-tuple-element.120, bf16[1024,4,32]{0,2,1:T(8,128)(2,1)S(1)} %get-tuple-element.119, s32[]{:T(128)S(6)} %select_n.27), kind=kOutput, calls=%fused_computation.7.clone.1 | convolution fusion | flops 276892672 | bytes 794628 | tf_op jit(solution)/shard_map/while/body/eval_jaxpr/hqk,khc->qhc/dot_general | solution.py:44
  96.7 3.0 %fusion.86 = f32[4,512]{1,0:T(4,128)S(1)} fusion(bf16[1024,4,32]{0,2,1:T(8,128)(2,1)S(1)} %get-tuple-element.120, bf16[1024,4,32]{0,2,1:T(8,128)(2,1)S(1)} %get-tuple-element.119, s32[]{:T(128)S(6)} %select_n.27), kind=kOutput, calls=%fused_computation.43.clone.1 | convolution fusion | flops 140510208 | bytes 401412 | tf_op jit(solution)/shard_map/while/body/eval_jaxpr/sub | solution.py:42
  99.6 3.1 %fusion.87 = bf16[4,512,32]{1,2,0:T(8,128)(2,1)S(1)} fusion(bf16[1024,4,32]{0,2,1:T(8,128)(2,1)S(1)} %get-tuple-element.121, f32[4,512]{1,0:T(4,128)S(1)} %fusion.86, bf16[1024,4,32]{0,2,1:T(8,128)(2,1)S(1)} %get-tuple-element.120, bf16[1024,4,32]{0,2,1:T(8,128)(2,1)S(1)} %get-tuple-element.119, s32[]{:T(128)S(6)} %select_n.27), kind=kOutput, calls=%fused_computation.7.clone.1 | convolution fusion | flops 276892672 | bytes 794628 | tf_op jit(solution)/shard_map/while/body/eval_jaxpr/hqk,khc->qhc/dot_general | solution.py:44
  103.6 3.4 %all-to-all-start.1 = ((bf16[8,128,128]{2,1,0:T(8,128)(2,1)}), bf16[8,128,128]{2,1,0:T(8,128)(2,1)S(1)}, u32[]{:S(2)}, u32[]{:S(2)}) async-start(bf16[8,128,128]{2,1,0:T(8,128)(2,1)} %bitcast.55), calls=%async_computation.1 | async-start | bytes 524288 | tf_op jit(solution)/shard_map/all_to_all | solution.py:92
  107.1 2.3 %convolution_add_fusion.3 = f32[128,1024]{1,0:T(8,128)S(1)} fusion(bf16[1024,1024]{1,0:T(8,128)(2,1)} %all-gather.4.cloned.1.call-done, f32[128,1024]{1,0:T(8,128)S(1)} %fusion.52, f32[128,1024]{1,0:T(8,128)S(1)} %convolution_add_fusion.1, bf16[32,1024]{1,0:T(8,128)(2,1)S(1)} %collective-permute-done, bf16[128,1024]{1,0:T(8,128)(2,1)S(1)} %copy-done, ...), kind=kOutput, calls=%fused_computation.26 | convolution fusion | flops 277618688 | bytes 4014624 | tf_op jit(solution)/shard_map/dot_general | solution.py:52
  109.3 4.5 %all-to-all-done.1 = bf16[8,128,128]{2,1,0:T(8,128)(2,1)S(1)} async-done(((bf16[8,128,128]{2,1,0:T(8,128)(2,1)}), bf16[8,128,128]{2,1,0:T(8,128)(2,1)S(1)}, u32[]{:S(2)}, u32[]{:S(2)}) %all-to-all-start.1) | async-done | bytes 262176 | tf_op jit(solution)/shard_map/all_to_all | solution.py:92
  114.1 8.5 %all-gather.8.cloned.1.call-done = bf16[1024,1024]{1,0:T(8,128)(2,1)} async-done(((bf16[128,1024]{1,0:T(8,128)(2,1)}), bf16[1024,1024]{1,0:T(8,128)(2,1)}) %all-gather.8.cloned.1.call-update) | async-done | bytes 2097168 | tf_op jit(solution)/shard_map/all_gather | solution.py:96
  122.6 2.8 %fusion.48 = bf16[128,1024]{1,0:T(8,128)(2,1)} fusion(f32[128,1024]{1,0:T(8,128)S(1)} %convolution_add_fusion.3, bf16[128,1024]{0,1:T(8,128)(2,1)S(1)} %bitcast.53, bf16[1024,1024]{1,0:T(8,128)(2,1)} %all-gather.8.cloned.1.call-done), kind=kOutput, calls=%fused_computation.28 | convolution fusion | flops 268697600 | bytes 3145728 | tf_op jit(solution)/shard_map/dot_general | solution.py:94
  (44 shorter events, 6.4 us)
Async XLA Ops:
  6.5 51.0 %all-gather.6.cloned.1.call-start = ((), (), s32[]{:S(2)}) async-start(), calls=%async_computation.3 | async-start | bytes 7077888 | tf_op jit(solution)/shard_map/all_gather | solution.py:87
  8.8 58.5 %copy-start = (bf16[128,1024]{1,0:T(8,128)(2,1)S(1)}, bf16[128,1024]{1,0:T(8,128)(2,1)}, u32[]{:S(2)}) copy-start(bf16[128,1024]{1,0:T(8,128)(2,1)} %param.10) | copy-start | bytes 786436
  8.9 58.5 %copy-start.3 = (s32[128,128]{1,0:T(8,128)S(1)}, s32[128,128]{1,0:T(8,128)}, u32[]{:S(2)}) copy-start(s32[128,128]{1,0:T(8,128)} %param.11) | copy-start | bytes 196612
  8.9 98.2 %all-gather.4.cloned.1.call-start = ((), (), s32[]{:S(2)}) async-start(), calls=%async_computation.2 | async-start | bytes 2359296 | tf_op jit(solution)/shard_map/all_gather | solution.py:53
  9.6 113.0 %all-gather.8.cloned.1.call-start = ((), (), s32[]{:S(2)}) async-start(), calls=%async_computation.4 | async-start | bytes 2359296 | tf_op jit(solution)/shard_map/all_gather | solution.py:96
  10.4 57.2 %copy-start.4 = (s32[128,32]{0,1:T(8,128)S(1)}, s32[128,32]{0,1:T(8,128)}, u32[]{:S(2)}) copy-start(s32[128,32]{0,1:T(8,128)} %param.13) | copy-start | bytes 49156
  11.3 56.3 %collective-permute-start.1 = (bf16[32,1024]{1,0:T(8,128)(2,1)S(1)}, bf16[32,1024]{1,0:T(8,128)(2,1)S(1)}, u32[]{:S(2)}, u32[]{:S(2)}) collective-permute-start(bf16[32,1024]{1,0:T(8,128)(2,1)S(1)} %get-tuple-element.54), channel_id=1, source_target_pairs={{1,0},{2,1},{3,2},{4,3},{5,4},{6,5},{7,6},{9,8},{10,9},{11,10},{12... | collective-permute-start | bytes 196616 | tf_op jit(solution)/shard_map/ppermute | solution.py:21
  12.6 94.5 %collective-permute-start = (bf16[32,1024]{1,0:T(8,128)(2,1)S(1)}, bf16[32,1024]{1,0:T(8,128)(2,1)S(1)}, u32[]{:S(2)}, u32[]{:S(2)}) collective-permute-start(bf16[32,1024]{1,0:T(8,128)(2,1)S(1)} %get-tuple-element.53), channel_id=1, source_target_pairs={{0,1},{1,2},{2,3},{3,4},{4,5},{5,6},{6,7},{8,9},{9,10},{10,11},{11... | collective-permute-start | bytes 196616 | tf_op jit(solution)/shard_map/ppermute | solution.py:19
  63.7 20.8 %all-to-all-start = ((bf16[3,128,1024]{1,0,2:T(4,128)(2,1)}), bf16[3,128,1024]{1,0,2:T(4,128)(2,1)S(1)}, u32[]{:S(2)}, u32[]{:S(2)}) async-start(bf16[3,128,1024]{1,0,2:T(4,128)(2,1)} %copy.20), calls=%async_computation | async-start | bytes 2097152 | tf_op jit(solution)/shard_map/all_to_all | solution.py:90
  87.0 20.1 %copy-start.5 = (s32[128,32]{0,1:T(8,128)S(1)}, s32[128,32]{0,1:T(8,128)}, u32[]{:S(2)}) copy-start(s32[128,32]{0,1:T(8,128)} %param.12) | copy-start | bytes 49156
  91.3 3.2 %copy-start.1 = (bf16[2,512,128]{2,1,0:T(8,128)(2,1)S(1)}, bf16[2,512,128]{2,1,0:T(8,128)(2,1)}, u32[]{:S(2)}) copy-start(bf16[2,512,128]{2,1,0:T(8,128)(2,1)} %get-tuple-element.107) | copy-start | bytes 786436 | tf_op jit(solution)/shard_map/while
  94.6 0.7 copy-start.2
  99.6 3.2 %copy-start.1 = (bf16[2,512,128]{2,1,0:T(8,128)(2,1)S(1)}, bf16[2,512,128]{2,1,0:T(8,128)(2,1)}, u32[]{:S(2)}) copy-start(bf16[2,512,128]{2,1,0:T(8,128)(2,1)} %get-tuple-element.107) | copy-start | bytes 786436 | tf_op jit(solution)/shard_map/while
  102.9 0.7 copy-start.2
  103.6 10.3 %all-to-all-start.1 = ((bf16[8,128,128]{2,1,0:T(8,128)(2,1)}), bf16[8,128,128]{2,1,0:T(8,128)(2,1)S(1)}, u32[]{:S(2)}, u32[]{:S(2)}) async-start(bf16[8,128,128]{2,1,0:T(8,128)(2,1)} %bitcast.55), calls=%async_computation.1 | async-start | bytes 524288 | tf_op jit(solution)/shard_map/all_to_all | solution.py:92
Sparse Core Ops, SparseCore 0:
  9.3 48.2 all-gather.5
  59.4 33.3 all-gather.3
  94.7 27.8 all-gather.7
where the time goes:
time: 133 us; the launch traced here: 132 us
  waiting for transfers between devices  68.5 us (52%)
  matrix products  22.2 us (17%)
  between operations  14 us (11%)
  local copies, waits for them, and re-layouts  11.9 us (9%)
  starting transfers between devices  11.4 us (9%)
  other arithmetic  2.41 us (2%)
  loops' own time  1.49 us (1%)
    all_gather x1, waiting for transfers between devices, body(): lax.all_gather(wqkv, 'dom', axis=2, tiled=True)  37.4 us
    all_to_all x1, waiting for transfers between devices, body(): lax.all_to_all(node_qkv, 'dom', split_axis=2, concat_axis=1, tiled=True)  16.6 us
    all_gather x1, waiting for transfers between devices, body(): lax.all_gather(w_out, 'dom', axis=0, tiled=True)  8.53 us
    dot_general x2, matrix products, one_block(): jnp.einsum('hqk,khc->qhc', weight, value, preferred_element_type=jnp.floa...  6.18 us
    sub x2, matrix products, one_block(): expo = jnp.exp(score - peak)  5.91 us
    dot_general x1, matrix products, body(): jnp.einsum('nd,tdc->tnc', feats, lax.all_gather(wqkv, 'dom', axis=2, tile...  4.59 us
    all_to_all x1, waiting for transfers between devices, body(): lax.all_to_all(head_out, 'dom', split_axis=0, concat_axis=1, tiled=True)  4.54 us
    all_to_all x1, starting transfers between devices, body(): lax.all_to_all(node_qkv, 'dom', split_axis=2, concat_axis=1, tiled=True)  3.56 us
  transfers between devices with their start and end apart: 7, of which 4 were waited for; matrix products, arithmetic and copies ran while one was open for 23% of the time, Pallas kernels for 0%

commit v1 on v0

--- a/solution.py
+++ b/solution.py
@@ -1,8 +1,11 @@
+import functools
 import math
 
 import jax
 import jax.numpy as jnp
 from jax import lax
+from jax.experimental import pallas as pl
+from jax.experimental.pallas import tpu as pltpu
 from jax.sharding import PartitionSpec as P
 
 HEADS = 32
@@ -99,6 +102,257 @@
     return (feats.astype(jnp.float32) + local + attn).astype(jnp.bfloat16)
 
 
+def layer_kernel(
+    parts, head_size,
+    feats, adj_own, adj_prev, adj_next, bcount, wqkv, w_mp, w_out, out,
+    fall, wcat, w2, qs, kt, v1, ms, mr, lhs, keep, sib_out, sib_in, rs_out, rs_in,
+    ag_send, ag_recv, mx_send, mx_recv, sb_send, sb_recv, rs_send, rs_recv,
+):
+    rows, width = feats.shape
+    cols = w_out.shape[0]
+    band = adj_prev.shape[1]
+    half = rows // 2
+    pair = 2 * rows
+    heads = cols // head_size
+    me = lax.axis_index("dom")
+    core = me % 2
+    chip = me // 2
+    sib = me + 1 - 2 * core
+    cx, cy = chip % 2, chip // 2
+
+    def chip_at(dx, dy):
+        return ((cy + dy) % 2) * 2 + (cx + dx) % 2
+
+    x_chip, y_chip, d_chip = chip_at(1, 0), chip_at(0, 1), chip_at(1, 1)
+    x_dev, y_dev, d_dev = x_chip * 2 + core, y_chip * 2 + core, d_chip * 2 + core
+    mesh_id = pl.DeviceIdType.MESH
+
+    def remote(src, dst, send_sem, recv_sem, dev):
+        return pltpu.make_async_remote_copy(
+            src_ref=src, dst_ref=dst, send_sem=send_sem, recv_sem=recv_sem,
+            device_id={"dom": dev}, device_id_type=mesh_id,
+        )
+
+    barrier = pltpu.get_barrier_semaphore()
+    for k in range(1, parts):
+        pl.semaphore_signal(barrier, inc=1, device_id={"dom": (me + k) % parts}, device_id_type=mesh_id)
+    pl.semaphore_wait(barrier, parts - 1)
+
+    started = []
+
+    def send_half(block, h, dev, own=False):
+        span = pl.ds(half * h, half)
+        dst = fall.at[block, span]
+        src = feats.at[span] if own else dst
+        copy = remote(src, dst, ag_send.at[len(started)], ag_recv.at[block, h], dev)
+        copy.start()
+        started.append(copy)
+
+    def wait_half(block, h):
+        dst = fall.at[block, pl.ds(half * h, half)]
+        remote(dst, dst, ag_send.at[0], ag_recv.at[block, h], sib).wait_recv()
+
+    send_half(me, 0, x_dev, True)
+    send_half(me, 1, y_dev, True)
+    send_half(me, 0, sib, True)
+    send_half(me, 1, sib, True)
+    send_half(me, 1, x_dev, True)
+    send_half(me, 0, y_dev, True)
+
+    fall[me] = feats[...]
+    for t in range(3):
+        wcat[:, t * cols : (t + 1) * cols] = wqkv[t]
+    w2[:cols] = w_out[...]
+    w2[cols:] = w_mp[...]
+    v1[:, cols:] = jnp.ones_like(v1[:, cols:])
+    lane_head = lax.broadcasted_iota(jnp.int32, (1, cols), 1) // head_size
+    factor = math.log2(math.e) / head_size**0.5
+
+    def project(c):
+        base = pl.multiple_of(c * pair, pair)
+        block = fall[pl.ds(2 * c, 2)].reshape(pair, width)
+        r = jnp.dot(block, wcat[...], preferred_element_type=jnp.float32)
+        q = r[:, :cols] * factor
+        for h in range(heads):
+            qs[h, pl.ds(base, pair), :] = jnp.where(lane_head == h, q, 0.0).astype(jnp.bfloat16)
+        kt[:, pl.ds(base, pair)] = r[:, cols : 2 * cols].T.astype(jnp.bfloat16)
+        v1[pl.ds(base, pair), :cols] = r[:, 2 * cols :].astype(jnp.bfloat16)
+
+    def wait_sib(c):
+        for h in range(2):
+            wait_half(2 * c + 1 - core, h)
+
+    wait_sib(chip)
+    project(chip)
+    wait_half(x_dev, 0)
+    send_half(x_dev, 0, y_dev)
+    send_half(x_dev, 0, sib)
+    wait_half(y_dev, 1)
+    send_half(y_dev, 1, x_dev)
+    send_half(y_dev, 1, sib)
+    wait_half(x_dev, 1)
+    send_half(x_dev, 1, sib)
+    wait_half(y_dev, 0)
+    send_half(y_dev, 0, sib)
+    wait_sib(x_chip)
+    project(x_chip)
+    wait_half(d_dev, 0)
+    send_half(d_dev, 0, sib)
+    wait_half(d_dev, 1)
+    send_half(d_dev, 1, sib)
+    wait_sib(y_chip)
+    project(y_chip)
+    wait_sib(d_chip)
+
+    before, after = (me + parts - 1) % parts, (me + 1) % parts
+    column = lax.broadcasted_iota(jnp.int32, (1, band), 1)
+    prev_count = jnp.where(me > 0, bcount[before, 1], 0)
+    next_count = jnp.where(me < parts - 1, bcount[after, 0], 0)
+    own = adj_own[...].astype(jnp.float32)
+    prv = jnp.where(column >= band - prev_count, adj_prev[...], 0).astype(jnp.float32)
+    nxt = jnp.where(column < next_count, adj_next[...], 0).astype(jnp.float32)
+    degree = (
+        1.0
+        + jnp.sum(own, -1, keepdims=True)
+        + jnp.sum(prv, -1, keepdims=True)
+        + jnp.sum(nxt, -1, keepdims=True)
+    )
+    total = feats[...].astype(jnp.float32)
+    total += jnp.dot(own.astype(jnp.bfloat16), feats[...], preferred_element_type=jnp.float32)
+    total += jnp.dot(
+        prv.astype(jnp.bfloat16), fall[before, rows - band :, :], preferred_element_type=jnp.float32
+    )
+    total += jnp.dot(
+        nxt.astype(jnp.bfloat16), fall[after, :band, :], preferred_element_type=jnp.float32
+    )
+    mixed = (total / degree).astype(jnp.bfloat16)
+    for j in range(parts):
+        ms[j] = mixed[:, j * cols : (j + 1) * cols]
+    mix_copies = []
+    for k in range(1, parts):
+        to = (me + k) % parts
+        copy = remote(ms.at[to], mr.at[me], mx_send.at[k], mx_recv.at[me], to)
+        copy.start()
+        mix_copies.append(copy)
+    mr[me] = ms[me]
+    project(d_chip)
+
+    def attention(c):
+        base = pl.multiple_of(c * pair, pair)
+        result = jnp.zeros((pair, cols), jnp.float32)
+        for h in range(heads):
+            score = jnp.dot(
+                qs[h, pl.ds(base, pair), :], kt[...], preferred_element_type=jnp.float32
+            )
+            peak = jnp.max(score, -1, keepdims=True)
+            weight = jnp.exp2(score - peak).astype(jnp.bfloat16)
+            both = jnp.dot(weight, v1[...], preferred_element_type=jnp.float32)
+            result = jnp.where(lane_head == h, both[:, :cols] / both[:, cols:], result)
+        lhs[:, :, :cols] = result.astype(jnp.bfloat16).reshape(2, rows, cols)
+
+    def partial_sums(slot, c):
+        lhs[:, :, cols:] = mr[pl.ds(2 * c, 2)]
+        sib_out[slot] = jnp.dot(
+            lhs[1 - core], w2[...], preferred_element_type=jnp.float32
+        ).astype(jnp.bfloat16)
+        to_sib(slot).start()
+        keep[slot] = jnp.dot(lhs[core], w2[...], preferred_element_type=jnp.float32)
+
+    def to_sib(slot):
+        return remote(sib_out.at[slot], sib_in.at[slot], sb_send.at[slot], sb_recv.at[slot], sib)
+
+    def to_chip(slot):
+        c = chip_at((slot + 1) % 2, (slot + 1) // 2)
+        return remote(
+            rs_out.at[slot], rs_in.at[slot], rs_send.at[slot], rs_recv.at[slot], c * 2 + core
+        )
+
+    def combine(slot):
+        to_sib(slot).wait_recv()
+        rs_out[slot] = (keep[slot] + sib_in[slot].astype(jnp.float32)).astype(jnp.bfloat16)
+        to_chip(slot).start()
+
+    attention(d_chip)
+    for k in range(1, parts):
+        source = (me + k) % parts
+        remote(ms.at[source], mr.at[source], mx_send.at[0], mx_recv.at[source], sib).wait_recv()
+    partial_sums(2, d_chip)
+
+    def step(i, _):
+        slot = 1 - i
+        c = chip_at((slot + 1) % 2, (slot + 1) // 2)
+        attention(c)
+        combine(slot + 1)
+        partial_sums(slot, c)
+        return 0
+
+    lax.fori_loop(0, 2, step, 0)
+    attention(chip)
+    combine(0)
+    partial_sums(3, chip)
+    final = feats[...].astype(jnp.float32) + keep[3]
+    to_sib(3).wait_recv()
+    final += sib_in[3].astype(jnp.float32)
+    for slot in (2, 1, 0):
+        to_chip(slot).wait_recv()
+        final += rs_in[slot].astype(jnp.float32)
+    out[...] = final.astype(out.dtype)
+    for copy in started:
+        copy.wait_send()
+    for copy in mix_copies:
+        copy.wait_send()
+    for slot in range(4):
+        to_sib(slot).wait_send()
+    for slot in range(3):
+        to_chip(slot).wait_send()
+
+
+def fused_layer(feats, adj_own, adj_prev, adj_next, bcount, wqkv, w_mp, w_out):
+    rows, width = feats.shape
+    cols = w_out.shape[0]
+    parts = lax.axis_size("dom")
+    nodes = rows * parts
+    head_size = width // HEADS
+    heads = cols // head_size
+    vmem = pl.BlockSpec(memory_space=pltpu.VMEM)
+    smem = pl.BlockSpec(memory_space=pltpu.SMEM)
+    bf16, f32 = jnp.bfloat16, jnp.float32
+    dma = pltpu.SemaphoreType.DMA
+    return pl.pallas_call(
+        functools.partial(layer_kernel, parts, head_size),
+        out_shape=jax.ShapeDtypeStruct((rows, width), bf16),
+        in_specs=[vmem, vmem, vmem, vmem, smem, vmem, vmem, vmem],
+        out_specs=vmem,
+        scratch_shapes=[
+            pltpu.VMEM((parts, rows, width), bf16),
+            pltpu.VMEM((width, 3 * cols), bf16),
+            pltpu.VMEM((2 * cols, width), bf16),
+            pltpu.VMEM((heads, nodes, cols), bf16),
+            pltpu.VMEM((cols, nodes), bf16),
+            pltpu.VMEM((nodes, 2 * cols), bf16),
+            pltpu.VMEM((parts, rows, cols), bf16),
+            pltpu.VMEM((parts, rows, cols), bf16),
+            pltpu.VMEM((2, rows, 2 * cols), bf16),
+            pltpu.VMEM((4, rows, width), f32),
+            pltpu.VMEM((4, rows, width), bf16),
+            pltpu.VMEM((4, rows, width), bf16),
+            pltpu.VMEM((3, rows, width), bf16),
+            pltpu.VMEM((3, rows, width), bf16),
+            dma((14,)),
+            dma((parts, 2)),
+            dma((parts,)),
+            dma((parts,)),
+            dma((4,)),
+            dma((4,)),
+            dma((3,)),
+            dma((3,)),
+        ],
+        compiler_params=pltpu.CompilerParams(
+            collective_id=0, has_side_effects=True, vmem_limit_bytes=48 * 1024 * 1024
+        ),
+    )(feats, adj_own, adj_prev, adj_next, bcount, wqkv, w_mp, w_out)
+
+
 def solution(mesh):
     placed = (
         P(("dp", "dom"), None),
@@ -110,6 +364,7 @@
         P("dom", None),
         P("dom", None),
     )
+    layer = fused_layer if mesh.shape["dom"] == 8 else body
     return jax.shard_map(
-        body, mesh=mesh, in_specs=placed, out_specs=P(("dp", "dom"), None), check_vma=False
-    )
+        layer, mesh=mesh, in_specs=placed, out_specs=P(("dp", "dom"), None), check_vma=False
+    )

time: 133 us -> 44.4 us (0.33)
  waiting for transfers between devices: 68.5 us -> 0 us
  Pallas kernels: 0 us -> 37.7 us
  matrix products: 22.2 us -> 0 us
  between operations: 14 us -> 0.04 us
  starting transfers between devices: 11.4 us -> 0 us
  local copies, waits for them, and re-layouts: 11.9 us -> 6.38 us
  other arithmetic: 2.41 us -> 0 us
  loops' own time: 1.49 us -> 0 us
    all_gather x3 -> x0, waiting for transfers between devices: 46 us -> none  [the longest x1 37.4 us: body(): lax.all_gather(wqkv, 'dom', axis=2, tiled=True)]
    pallas_call x0 -> x1, Pallas kernels: none -> 37.7 us  [fused_layer(): pl.pallas_call(functools.partial(layer_kernel, parts, head_size), out_sha...]
    all_to_all x2 -> x0, waiting for transfers between devices: 21.1 us -> none  [the longest x1 16.6 us: body(): lax.all_to_all(node_qkv, 'dom', split_axis=2, concat_axis=1, tiled=True)]
    dot_general x7 -> x0, matrix products: 16.3 us -> none  [the longest x2 6.18 us: one_block(): jnp.einsum('hqk,khc->qhc', weight, value, preferred_element_type=jnp.floa...]
    all_to_all x2 -> x0, starting transfers between devices: 6.98 us -> none  [the longest x1 3.56 us: body(): lax.all_to_all(node_qkv, 'dom', split_axis=2, concat_axis=1, tiled=True)]
    sub x2 -> x0, matrix products: 5.91 us -> none  [one_block(): expo = jnp.exp(score - peak)]
    ppermute x2 -> x0, starting transfers between devices: 4.33 us -> none  [the longest x1 3.03 us: with_halo(): lax.ppermute(tail, axis, [(i, (i + 1) % count) for i in range(ends)])]
    unnamed x9 -> x16, local copies, waits for them, and re-layouts: 2.31 us -> 6.38 us
  transfers between devices with their start and end apart: 7 -> 0, of which waited for: 4 -> 0; matrix products, arithmetic and copies ran while one was open for 23% -> 0% of each run, Pallas kernels for 0% -> 0%
where the time goes in v1:
time: 44.4 us; the launch traced here: 44.1 us
  Pallas kernels  37.7 us (85%)
  local copies, waits for them, and re-layouts  6.38 us (14%)
    pallas_call x1, Pallas kernels, fused_layer(): pl.pallas_call(functools.partial(layer_kernel, parts, head_size), out_sha...  37.7 us
    unnamed x16, local copies, waits for them, and re-layouts  6.38 us

profile of v1, /device:TPU:0, one launch (start us, length us, event | category | flops | bytes accessed | tf_op | source)
XLA Modules:
  0.0 44.1 jit_solution(261290893827463281)
XLA Ops:
  0.0 0.8 %copy.11.bcount = s32[8,2]{1,0:T(8,128)S(1)} copy(s32[8,2]{0,1:T(2,128)} %param.12) | data formatting | bytes 128 | tf_op args[4]
  0.8 0.0 copy-start.5
  0.8 0.0 copy-start.4
  0.8 0.8 %copy.9.adj_prev = s32[128,32]{1,0:T(8,128)S(1)} copy(s32[128,32]{0,1:T(8,128)} %param.10) | data formatting | bytes 32768 | tf_op args[2]
  1.6 0.0 copy-done.5
  1.6 0.1 copy.10.adj_next
  1.7 0.0 copy-done.4
  1.7 0.0 copy-start
  1.7 1.1 %copy-done = bf16[3,1024,128]{2,1,0:T(8,128)(2,1)S(1)} copy-done((bf16[3,1024,128]{2,1,0:T(8,128)(2,1)S(1)}, bf16[3,1024,128]{2,1,0:T(8,128)(2,1)}, u32[]{:S(2)}) %copy-start) | copy-done | bytes 786456
  2.9 0.0 copy-start.1
  2.9 0.9 %copy-done.1 = bf16[128,1024]{1,0:T(8,128)(2,1)S(1)} copy-done((bf16[128,1024]{1,0:T(8,128)(2,1)S(1)}, bf16[128,1024]{1,0:T(8,128)(2,1)}, u32[]{:S(2)}) %copy-start.1) | copy-done | bytes 262168
  3.8 0.0 copy-start.2
  3.8 0.9 %copy-done.2 = bf16[128,1024]{1,0:T(8,128)(2,1)S(1)} copy-done((bf16[128,1024]{1,0:T(8,128)(2,1)S(1)}, bf16[128,1024]{1,0:T(8,128)(2,1)}, u32[]{:S(2)}) %copy-start.2) | copy-done | bytes 262168
  4.8 0.0 copy-start.3
  4.8 0.9 %copy-done.3 = bf16[128,1024]{1,0:T(8,128)(2,1)S(1)} copy-done((bf16[128,1024]{1,0:T(8,128)(2,1)S(1)}, bf16[128,1024]{1,0:T(8,128)(2,1)}, u32[]{:S(2)}) %copy-start.3) | copy-done | bytes 262168
  5.7 37.7 %shard_map.82 = bf16[128,1024]{1,0:T(8,128)(2,1)S(1)} custom-call(bf16[128,1024]{1,0:T(8,128)(2,1)S(1)} %copy-done.1, s32[128,128]{1,0:T(8,128)S(1)} %copy-done.4, s32[128,32]{1,0:T(8,128)S(1)} %copy.9.adj_prev, s32[128,32]{1,0:T(8,128)S(1)} %copy.10.adj_next, s32[8,2]{1,0:T(8,128)S(1)} %copy.11.bcount, bf16[3,1024,128]{2,1,0:T(8,128)(2,1)S(1)} %copy-done, ...), custom_call_target="tpu_custom_call" | custom-call | tf_op jit(solution)/shard_map/pallas_call | solution.py:321
  43.4 0.7 %copy.13 = bf16[128,1024]{1,0:T(8,128)(2,1)} copy(bf16[128,1024]{1,0:T(8,128)(2,1)S(1)} %shard_map.82) | data formatting | bytes 524288
Async XLA Ops:
  0.8 0.9 %copy-start.5 = (s32[128,32]{0,1:T(8,128)S(1)}, s32[128,32]{0,1:T(8,128)}, u32[]{:S(2)}) copy-start(s32[128,32]{0,1:T(8,128)} %param.11) | copy-start | bytes 49156
  0.8 1.0 %copy-start.4 = (s32[128,128]{1,0:T(8,128)S(1)}, s32[128,128]{1,0:T(8,128)}, u32[]{:S(2)}) copy-start(s32[128,128]{1,0:T(8,128)} %adj_own.1) | copy-start | bytes 196612
  1.7 1.1 %copy-start = (bf16[3,1024,128]{2,1,0:T(8,128)(2,1)S(1)}, bf16[3,1024,128]{2,1,0:T(8,128)(2,1)}, u32[]{:S(2)}) copy-start(bf16[3,1024,128]{2,1,0:T(8,128)(2,1)} %wqkv.1) | copy-start | bytes 2359300
  2.9 0.9 %copy-start.1 = (bf16[128,1024]{1,0:T(8,128)(2,1)S(1)}, bf16[128,1024]{1,0:T(8,128)(2,1)}, u32[]{:S(2)}) copy-start(bf16[128,1024]{1,0:T(8,128)(2,1)} %feats.1) | copy-start | bytes 786436
  3.8 0.9 %copy-start.2 = (bf16[128,1024]{1,0:T(8,128)(2,1)S(1)}, bf16[128,1024]{1,0:T(8,128)(2,1)}, u32[]{:S(2)}) copy-start(bf16[128,1024]{1,0:T(8,128)(2,1)} %w_mp.1) | copy-start | bytes 786436
  4.8 0.9 %copy-start.3 = (bf16[128,1024]{1,0:T(8,128)(2,1)S(1)}, bf16[128,1024]{1,0:T(8,128)(2,1)}, u32[]{:S(2)}) copy-start(bf16[128,1024]{1,0:T(8,128)(2,1)} %w_out.1) | copy-start | bytes 786436

commit v2 on v1

--- a/solution.py
+++ b/solution.py
@@ -105,12 +105,13 @@
 def layer_kernel(
     parts, head_size,
     feats, adj_own, adj_prev, adj_next, bcount, wqkv, w_mp, w_out, out,
-    fall, wcat, w2, qs, kt, v1, ms, mr, lhs, keep, sib_out, sib_in, rs_out, rs_in,
-    ag_send, ag_recv, mx_send, mx_recv, sb_send, sb_recv, rs_send, rs_recv,
+    fall, own_adj, prev_adj, next_adj, counts, wcat, w2, qs, kt, v1, ms, mr, lhs, keep,
+    sib_out, sib_in, rs_out, rs_in, relay_in,
+    load_sem, ag_send, ag_recv, mx_send, mx_recv, sb_send, sb_recv, rs_send, rs_recv,
 ):
     rows, width = feats.shape
     cols = w_out.shape[0]
-    band = adj_prev.shape[1]
+    band = adj_prev.shape[0]
     half = rows // 2
     pair = 2 * rows
     heads = cols // head_size
@@ -133,6 +134,14 @@
             device_id={"dom": dev}, device_id_type=mesh_id,
         )
 
+    pairs = [(feats, fall.at[me])]
+    pairs += [(wqkv.at[t], wcat.at[:, pl.ds(t * cols, cols)]) for t in range(3)]
+    pairs += [(adj_own, own_adj), (adj_prev, prev_adj), (adj_next, next_adj), (bcount, counts)]
+    pairs += [(w_out, w2.at[pl.ds(0, cols)]), (w_mp, w2.at[pl.ds(cols, cols)])]
+    loads = [pltpu.make_async_copy(a, b, load_sem.at[k]) for k, (a, b) in enumerate(pairs)]
+    for load in loads:
+        load.start()
+
     barrier = pltpu.get_barrier_semaphore()
     for k in range(1, parts):
         pl.semaphore_signal(barrier, inc=1, device_id={"dom": (me + k) % parts}, device_id_type=mesh_id)
@@ -159,11 +168,6 @@
     send_half(me, 1, x_dev, True)
     send_half(me, 0, y_dev, True)
 
-    fall[me] = feats[...]
-    for t in range(3):
-        wcat[:, t * cols : (t + 1) * cols] = wqkv[t]
-    w2[:cols] = w_out[...]
-    w2[cols:] = w_mp[...]
     v1[:, cols:] = jnp.ones_like(v1[:, cols:])
     lane_head = lax.broadcasted_iota(jnp.int32, (1, cols), 1) // head_size
     factor = math.log2(math.e) / head_size**0.5
@@ -182,6 +186,8 @@
         for h in range(2):
             wait_half(2 * c + 1 - core, h)
 
+    for load in loads:
+        load.wait()
     wait_sib(chip)
     project(chip)
     wait_half(x_dev, 0)
@@ -205,20 +211,23 @@
     wait_sib(d_chip)
 
     before, after = (me + parts - 1) % parts, (me + 1) % parts
-    column = lax.broadcasted_iota(jnp.int32, (1, band), 1)
-    prev_count = jnp.where(me > 0, bcount[before, 1], 0)
-    next_count = jnp.where(me < parts - 1, bcount[after, 0], 0)
-    own = adj_own[...].astype(jnp.float32)
-    prv = jnp.where(column >= band - prev_count, adj_prev[...], 0).astype(jnp.float32)
-    nxt = jnp.where(column < next_count, adj_next[...], 0).astype(jnp.float32)
+    column = lax.broadcasted_iota(jnp.int32, (band, 1), 0)
+    device = lax.broadcasted_iota(jnp.int32, (1, parts), 1)
+    prev_count = jnp.sum(jnp.where((device == before) & (me > 0), counts[1:2], 0), -1, keepdims=True)
+    next_count = jnp.sum(
+        jnp.where((device == after) & (me < parts - 1), counts[0:1], 0), -1, keepdims=True
+    )
+    own = own_adj[...].astype(jnp.float32)
+    prv = jnp.where(column >= band - prev_count, prev_adj[...], 0).astype(jnp.float32).T
+    nxt = jnp.where(column < next_count, next_adj[...], 0).astype(jnp.float32).T
     degree = (
         1.0
         + jnp.sum(own, -1, keepdims=True)
         + jnp.sum(prv, -1, keepdims=True)
         + jnp.sum(nxt, -1, keepdims=True)
     )
-    total = feats[...].astype(jnp.float32)
-    total += jnp.dot(own.astype(jnp.bfloat16), feats[...], preferred_element_type=jnp.float32)
+    total = fall[me].astype(jnp.float32)
+    total += jnp.dot(own.astype(jnp.bfloat16), fall[me], preferred_element_type=jnp.float32)
     total += jnp.dot(
         prv.astype(jnp.bfloat16), fall[before, rows - band :, :], preferred_element_type=jnp.float32
     )
@@ -229,82 +238,92 @@
     for j in range(parts):
         ms[j] = mixed[:, j * cols : (j + 1) * cols]
     mix_copies = []
-    for k in range(1, parts):
-        to = (me + k) % parts
+    others = [2 * c + k for c in (d_chip, x_chip, y_chip) for k in (1 - core, core)] + [sib]
+    for k, to in enumerate(others):
         copy = remote(ms.at[to], mr.at[me], mx_send.at[k], mx_recv.at[me], to)
         copy.start()
         mix_copies.append(copy)
     mr[me] = ms[me]
     project(d_chip)
 
-    def attention(c):
-        base = pl.multiple_of(c * pair, pair)
-        result = jnp.zeros((pair, cols), jnp.float32)
+    def attention(owner):
+        base = pl.multiple_of(owner * rows, rows)
+        result = jnp.zeros((rows, cols), jnp.float32)
         for h in range(heads):
             score = jnp.dot(
-                qs[h, pl.ds(base, pair), :], kt[...], preferred_element_type=jnp.float32
+                qs[h, pl.ds(base, rows), :], kt[...], preferred_element_type=jnp.float32
             )
             peak = jnp.max(score, -1, keepdims=True)
             weight = jnp.exp2(score - peak).astype(jnp.bfloat16)
             both = jnp.dot(weight, v1[...], preferred_element_type=jnp.float32)
             result = jnp.where(lane_head == h, both[:, :cols] / both[:, cols:], result)
-        lhs[:, :, :cols] = result.astype(jnp.bfloat16).reshape(2, rows, cols)
-
-    def partial_sums(slot, c):
-        lhs[:, :, cols:] = mr[pl.ds(2 * c, 2)]
-        sib_out[slot] = jnp.dot(
-            lhs[1 - core], w2[...], preferred_element_type=jnp.float32
-        ).astype(jnp.bfloat16)
-        to_sib(slot).start()
-        keep[slot] = jnp.dot(lhs[core], w2[...], preferred_element_type=jnp.float32)
+        lhs[:, :cols] = result.astype(jnp.bfloat16)
+
+    def partial_sum(owner, arrives=True):
+        attention(owner)
+        if arrives:
+            remote(mr.at[owner], mr.at[owner], mx_send.at[0], mx_recv.at[owner], sib).wait_recv()
+        lhs[:, cols:] = mr[owner]
+        return jnp.dot(lhs[...], w2[...], preferred_element_type=jnp.float32)
 
     def to_sib(slot):
         return remote(sib_out.at[slot], sib_in.at[slot], sb_send.at[slot], sb_recv.at[slot], sib)
 
-    def to_chip(slot):
-        c = chip_at((slot + 1) % 2, (slot + 1) // 2)
-        return remote(
-            rs_out.at[slot], rs_in.at[slot], rs_send.at[slot], rs_recv.at[slot], c * 2 + core
-        )
-
-    def combine(slot):
-        to_sib(slot).wait_recv()
-        rs_out[slot] = (keep[slot] + sib_in[slot].astype(jnp.float32)).astype(jnp.bfloat16)
-        to_chip(slot).start()
-
-    attention(d_chip)
-    for k in range(1, parts):
-        source = (me + k) % parts
-        remote(ms.at[source], mr.at[source], mx_send.at[0], mx_recv.at[source], sib).wait_recv()
-    partial_sums(2, d_chip)
-
-    def step(i, _):
-        slot = 1 - i
-        c = chip_at((slot + 1) % 2, (slot + 1) // 2)
-        attention(c)
-        combine(slot + 1)
-        partial_sums(slot, c)
-        return 0
-
-    lax.fori_loop(0, 2, step, 0)
-    attention(chip)
-    combine(0)
-    partial_sums(3, chip)
-    final = feats[...].astype(jnp.float32) + keep[3]
+    def unit(slot, c):
+        sib_out[slot] = partial_sum(2 * c + 1 - core).astype(jnp.bfloat16)
+        to_sib(slot).start()
+        keep[slot] = partial_sum(2 * c + core, arrives=slot < 3)
+
+    low, high = pl.ds(0, half), pl.ds(half, half)
+
+    def combined(slot, span, extra=None):
+        value = keep[slot, span] + sib_in[slot, span].astype(jnp.float32)
+        if extra is not None:
+            value += extra.astype(jnp.float32)
+        rs_out[slot, span] = value.astype(jnp.bfloat16)
+
+    x_relay = remote(rs_out.at[2, low], relay_in.at[0], rs_send.at[0], rs_recv.at[0], x_dev)
+    y_relay = remote(rs_out.at[2, high], relay_in.at[1], rs_send.at[1], rs_recv.at[1], y_dev)
+    x_low = remote(rs_out.at[0, low], rs_in.at[0, low], rs_send.at[2], rs_recv.at[2], x_dev)
+    x_high = remote(rs_out.at[0, high], rs_in.at[0, high], rs_send.at[3], rs_recv.at[3], x_dev)
+    y_low = remote(rs_out.at[1, low], rs_in.at[1, low], rs_send.at[4], rs_recv.at[4], y_dev)
+    y_high = remote(rs_out.at[1, high], rs_in.at[1, high], rs_send.at[5], rs_recv.at[5], y_dev)
+
+    unit(2, d_chip)
+    to_sib(2).wait_recv()
+    combined(2, low)
+    x_relay.start()
+    combined(2, high)
+    y_relay.start()
+    unit(0, x_chip)
+    to_sib(0).wait_recv()
+    combined(0, low)
+    x_low.start()
+    unit(1, y_chip)
+    to_sib(1).wait_recv()
+    combined(1, high)
+    y_high.start()
+    y_relay.wait_recv()
+    combined(0, high, relay_in[1])
+    x_high.start()
+    x_relay.wait_recv()
+    combined(1, low, relay_in[0])
+    y_low.start()
+    unit(3, chip)
+    final = fall[me].astype(jnp.float32) + keep[3]
     to_sib(3).wait_recv()
-    final += sib_in[3].astype(jnp.float32)
-    for slot in (2, 1, 0):
-        to_chip(slot).wait_recv()
-        final += rs_in[slot].astype(jnp.float32)
-    out[...] = final.astype(out.dtype)
-    for copy in started:
-        copy.wait_send()
-    for copy in mix_copies:
+    keep[3] = final + sib_in[3].astype(jnp.float32)
+    x_low.wait_recv()
+    y_high.wait_recv()
+    x_high.wait_recv()
+    y_low.wait_recv()
+    out[...] = (
+        keep[3] + rs_in[0].astype(jnp.float32) + rs_in[1].astype(jnp.float32)
+    ).astype(out.dtype)
+    for copy in started + mix_copies + [x_relay, y_relay, x_low, x_high, y_low, y_high]:
         copy.wait_send()
     for slot in range(4):
         to_sib(slot).wait_send()
-    for slot in range(3):
-        to_chip(slot).wait_send()
 
 
 def fused_layer(feats, adj_own, adj_prev, adj_next, bcount, wqkv, w_mp, w_out):
@@ -315,16 +334,20 @@
     head_size = width // HEADS
     heads = cols // head_size
     vmem = pl.BlockSpec(memory_space=pltpu.VMEM)
-    smem = pl.BlockSpec(memory_space=pltpu.SMEM)
+    hbm = pl.BlockSpec(memory_space=pltpu.HBM)
     bf16, f32 = jnp.bfloat16, jnp.float32
     dma = pltpu.SemaphoreType.DMA
     return pl.pallas_call(
         functools.partial(layer_kernel, parts, head_size),
         out_shape=jax.ShapeDtypeStruct((rows, width), bf16),
-        in_specs=[vmem, vmem, vmem, vmem, smem, vmem, vmem, vmem],
+        in_specs=[hbm] * 8,
         out_specs=vmem,
         scratch_shapes=[
             pltpu.VMEM((parts, rows, width), bf16),
+            pltpu.VMEM(adj_own.shape, adj_own.dtype),
+            pltpu.VMEM(adj_prev.shape[::-1], adj_prev.dtype),
+            pltpu.VMEM(adj_next.shape[::-1], adj_next.dtype),
+            pltpu.VMEM(bcount.shape[::-1], bcount.dtype),
             pltpu.VMEM((width, 3 * cols), bf16),
             pltpu.VMEM((2 * cols, width), bf16),
             pltpu.VMEM((heads, nodes, cols), bf16),
@@ -332,25 +355,27 @@
             pltpu.VMEM((nodes, 2 * cols), bf16),
             pltpu.VMEM((parts, rows, cols), bf16),
             pltpu.VMEM((parts, rows, cols), bf16),
-            pltpu.VMEM((2, rows, 2 * cols), bf16),
+            pltpu.VMEM((rows, 2 * cols), bf16),
             pltpu.VMEM((4, rows, width), f32),
             pltpu.VMEM((4, rows, width), bf16),
             pltpu.VMEM((4, rows, width), bf16),
             pltpu.VMEM((3, rows, width), bf16),
-            pltpu.VMEM((3, rows, width), bf16),
+            pltpu.VMEM((2, rows, width), bf16),
+            pltpu.VMEM((2, rows // 2, width), bf16),
+            dma((10,)),
             dma((14,)),
             dma((parts, 2)),
             dma((parts,)),
             dma((parts,)),
             dma((4,)),
             dma((4,)),
-            dma((3,)),
-            dma((3,)),
+            dma((6,)),
+            dma((6,)),
         ],
         compiler_params=pltpu.CompilerParams(
-            collective_id=0, has_side_effects=True, vmem_limit_bytes=48 * 1024 * 1024
+            collective_id=0, has_side_effects=True, vmem_limit_bytes=64 * 1024 * 1024
         ),
-    )(feats, adj_own, adj_prev, adj_next, bcount, wqkv, w_mp, w_out)
+    )(feats, adj_own, adj_prev.T, adj_next.T, bcount.T, wqkv, w_mp, w_out)
 
 
 def solution(mesh):

time: 44.4 us -> 37.3 us (0.84)
  local copies, waits for them, and re-layouts: 6.38 us -> 1.67 us
  Pallas kernels: 37.7 us -> 35.5 us
    unnamed x16 -> x1, local copies, waits for them, and re-layouts: 6.38 us -> 1.67 us
    pallas_call x1, Pallas kernels: 37.7 us -> 35.5 us  [fused_layer(): pl.pallas_call(functools.partial(layer_kernel, parts, head_size), out_sha...]
where the time goes in v2:
time: 37.3 us; the launch traced here: 37.1 us
  Pallas kernels  35.5 us (95%)
  local copies, waits for them, and re-layouts  1.67 us (4%)
    pallas_call x1, Pallas kernels, fused_layer(): pl.pallas_call(functools.partial(layer_kernel, parts, head_size), out_sha...  35.5 us
    unnamed x1, local copies, waits for them, and re-layouts  1.67 us

profile of v2, /device:TPU:0, one launch (start us, length us, event | category | flops | bytes accessed | tf_op | source)
XLA Modules:
  0.0 37.1 jit_solution(7432070792221958231)
XLA Ops:
  0.0 35.5 %shard_map.82 = bf16[128,1024]{1,0:T(8,128)(2,1)} custom-call(bf16[128,1024]{1,0:T(8,128)(2,1)} %feats.1, s32[128,128]{1,0:T(8,128)} %adj_own.1, s32[32,128]{1,0:T(8,128)} %bitcast.3, s32[32,128]{1,0:T(8,128)} %bitcast.4, s32[2,8]{1,0:T(2,128)} %bitcast.5, bf16[3,1024,128]{2,1,0:T(8,128)(2,1)} %wqkv.1, bf16[128,1024]{1,0:T(8,128)(2,1)} %w_mp.1, ...), custom_call_target="tpu_custom_call" | custom-call | tf_op jit(solution)/shard_map/pallas_call | solution.py:340
  35.5 1.7 %copy.10 = bf16[128,1024]{1,0:T(8,128)(2,1)} copy(bf16[128,1024]{1,0:T(8,128)(2,1)} %shard_map.82) | data formatting | bytes 524288

commit v3 on v2

--- a/solution.py
+++ b/solution.py
@@ -190,6 +190,24 @@
         load.wait()
     wait_sib(chip)
     project(chip)
+    before, after = (me + parts - 1) % parts, (me + 1) % parts
+    column = lax.broadcasted_iota(jnp.int32, (band, 1), 0)
+    device = lax.broadcasted_iota(jnp.int32, (1, parts), 1)
+    prev_count = jnp.sum(jnp.where((device == before) & (me > 0), counts[1:2], 0), -1, keepdims=True)
+    next_count = jnp.sum(
+        jnp.where((device == after) & (me < parts - 1), counts[0:1], 0), -1, keepdims=True
+    )
+    own = own_adj[...].astype(jnp.float32)
+    prv = jnp.where(column >= band - prev_count, prev_adj[...], 0).astype(jnp.float32).T
+    nxt = jnp.where(column < next_count, next_adj[...], 0).astype(jnp.float32).T
+    degree = (
+        1.0
+        + jnp.sum(own, -1, keepdims=True)
+        + jnp.sum(prv, -1, keepdims=True)
+        + jnp.sum(nxt, -1, keepdims=True)
+    )
+    total = fall[me].astype(jnp.float32)
+    total += jnp.dot(own.astype(jnp.bfloat16), fall[me], preferred_element_type=jnp.float32)
     wait_half(x_dev, 0)
     send_half(x_dev, 0, y_dev)
     send_half(x_dev, 0, sib)
@@ -210,24 +228,6 @@
     project(y_chip)
     wait_sib(d_chip)
 
-    before, after = (me + parts - 1) % parts, (me + 1) % parts
-    column = lax.broadcasted_iota(jnp.int32, (band, 1), 0)
-    device = lax.broadcasted_iota(jnp.int32, (1, parts), 1)
-    prev_count = jnp.sum(jnp.where((device == before) & (me > 0), counts[1:2], 0), -1, keepdims=True)
-    next_count = jnp.sum(
-        jnp.where((device == after) & (me < parts - 1), counts[0:1], 0), -1, keepdims=True
-    )
-    own = own_adj[...].astype(jnp.float32)
-    prv = jnp.where(column >= band - prev_count, prev_adj[...], 0).astype(jnp.float32).T
-    nxt = jnp.where(column < next_count, next_adj[...], 0).astype(jnp.float32).T
-    degree = (
-        1.0
-        + jnp.sum(own, -1, keepdims=True)
-        + jnp.sum(prv, -1, keepdims=True)
-        + jnp.sum(nxt, -1, keepdims=True)
-    )
-    total = fall[me].astype(jnp.float32)
-    total += jnp.dot(own.astype(jnp.bfloat16), fall[me], preferred_element_type=jnp.float32)
     total += jnp.dot(
         prv.astype(jnp.bfloat16), fall[before, rows - band :, :], preferred_element_type=jnp.float32
     )
@@ -248,7 +248,8 @@
 
     def attention(owner):
         base = pl.multiple_of(owner * rows, rows)
-        result = jnp.zeros((rows, cols), jnp.float32)
+        top = jnp.zeros((rows, cols), jnp.float32)
+        bottom = jnp.ones((rows, cols), jnp.float32)
         for h in range(heads):
             score = jnp.dot(
                 qs[h, pl.ds(base, rows), :], kt[...], preferred_element_type=jnp.float32
@@ -256,8 +257,9 @@
             peak = jnp.max(score, -1, keepdims=True)
             weight = jnp.exp2(score - peak).astype(jnp.bfloat16)
             both = jnp.dot(weight, v1[...], preferred_element_type=jnp.float32)
-            result = jnp.where(lane_head == h, both[:, :cols] / both[:, cols:], result)
-        lhs[:, :cols] = result.astype(jnp.bfloat16)
+            top = jnp.where(lane_head == h, both[:, :cols], top)
+            bottom = jnp.where(lane_head == h, both[:, cols:], bottom)
+        lhs[:, :cols] = (top / bottom).astype(jnp.bfloat16)
 
     def partial_sum(owner, arrives=True):
         attention(owner)

time: 37.3 us -> 37.1 us (level)
  no operation moved by 1% of the time
where the time goes in v3:
time: 37.1 us; the launch traced here: 37 us
  Pallas kernels  35.3 us (95%)
  local copies, waits for them, and re-layouts  1.67 us (5%)
    pallas_call x1, Pallas kernels, fused_layer(): pl.pallas_call(functools.partial(layer_kernel, parts, head_size), out_sha...  35.3 us
    unnamed x1, local copies, waits for them, and re-layouts  1.67 us

profile of v3, /device:TPU:0, one launch (start us, length us, event | category | flops | bytes accessed | tf_op | source)
XLA Modules:
  0.0 37.0 jit_solution(12248008320974875671)
XLA Ops:
  0.0 35.3 %shard_map.82 = bf16[128,1024]{1,0:T(8,128)(2,1)} custom-call(bf16[128,1024]{1,0:T(8,128)(2,1)} %feats.1, s32[128,128]{1,0:T(8,128)} %adj_own.1, s32[32,128]{1,0:T(8,128)} %bitcast.3, s32[32,128]{1,0:T(8,128)} %bitcast.4, s32[2,8]{1,0:T(2,128)} %bitcast.5, bf16[3,1024,128]{2,1,0:T(8,128)(2,1)} %wqkv.1, bf16[128,1024]{1,0:T(8,128)(2,1)} %w_mp.1, ...), custom_call_target="tpu_custom_call" | custom-call | tf_op jit(solution)/shard_map/pallas_call | solution.py:342
  35.3 1.7 %copy.10 = bf16[128,1024]{1,0:T(8,128)(2,1)} copy(bf16[128,1024]{1,0:T(8,128)(2,1)} %shard_map.82) | data formatting | bytes 524288
